TPU v7x, 1024 devices: a whole 4x4x32 slice. The times are simulated.
1024 devices in a mesh: energy: 64 (over z, core), momentum: 16 (over y, x).
Axes of the slice: x: 4, y: 4, z: 32, core: 2. Of those that a mesh axis runs over, the one named last changes fastest.
Arguments:
- green: bfloat16 [192, 16, 2, 384, 384], P('energy', 'momentum'), may hold values from -0.3125 to 0.3125
- contact: bfloat16 [192, 16, 2, 3, 128, 128], P('energy', 'momentum'), may hold values from -6 to 6
- tile_count: int32 [192], P('energy'), may hold values from 1 to 3
- offsets: int32 [3], replicated, may hold values from 1 to 3, as said below
- pair_index: int32 [3, 16, 16], replicated, may hold values from 0 to 15
- coupling_table: float32 [3, 16], replicated, may hold values from 0.05 to 0.3
Outputs:
- lesser_tiles: bfloat16 [192, 16, 2, 3, 128, 128], P('energy', 'momentum')
- self_energy: bfloat16 [192, 16, 2, 3, 128, 128], P('energy', 'momentum')
Inputs may be any that keep to these rules, and one draw needn't show every extreme that they name: `offsets`: the largest offset equals 3 in every draw.
All inputs are finite; a program needn't handle non-finite values.
Results may differ from a plain program's by a relative error of at most 0.009.
Values may be sent and summed in bfloat16 or wider, within the bound.
No kernel may reach another device: no remote copies, remote signals or barrier semaphores. Data moves between devices by JAX's collectives and lax.ppermute only.
A program may use at most 64 MiB of HBM per device.

v0:
```python
import jax
import jax.numpy as jnp
from jax import lax
from jax.sharding import PartitionSpec as P

OMAX = 3
ITERS = 2


def padded_2(block, sides, width):
    for axis, dim in sides:
        count = lax.axis_size(axis)
        forward = [(i, i + 1) for i in range(count - 1)]
        backward = [(target, source) for source, target in forward]
        low = lax.ppermute(
            lax.slice_in_dim(block, block.shape[dim] - width, None, axis=dim), axis, forward
        )
        high = lax.ppermute(lax.slice_in_dim(block, 0, width, axis=dim), axis, backward)
        block = jnp.concatenate([low, block, high], axis=dim)
    return block


def couplings(pair_index, coupling_table, count_table):
    hits = (pair_index[..., None] == jnp.arange(count_table, dtype=jnp.int32)).astype(jnp.float32)
    return jnp.einsum("mkqc,mc->mkq", hits, coupling_table, precision=lax.Precision.HIGHEST)


def lesser_onsite(blocks, sigma, counts):
    energies, order = (blocks.shape[0], blocks.shape[-1])
    tiles, width = (sigma.shape[2], sigma.shape[3])
    g_real = blocks[:, 0].reshape(energies, order, tiles, width)
    g_imag = blocks[:, 1].reshape(energies, order, tiles, width)
    s_real = sigma[:, 0]
    s_imag = sigma[:, 1]
    form = "ertc,etcd->ertd"
    polarization_real = jnp.einsum(
        form, g_real, s_real, preferred_element_type=jnp.float32
    ) - jnp.einsum(form, g_imag, s_imag, preferred_element_type=jnp.float32)
    polarization_imag = jnp.einsum(
        form, g_real, s_imag, preferred_element_type=jnp.float32
    ) + jnp.einsum(form, g_imag, s_real, preferred_element_type=jnp.float32)
    polarization_real = polarization_real.astype(jnp.bfloat16).reshape(
        energies, tiles, width, order
    )
    polarization_imag = polarization_imag.astype(jnp.bfloat16).reshape(
        energies, tiles, width, order
    )
    hamiltonian_real = blocks[:, 0].reshape(energies, tiles, width, order)
    hamiltonian_imag = blocks[:, 1].reshape(energies, tiles, width, order)
    pairs = "etab,etcb->etac"
    phonon_propagator_real = jnp.einsum(
        pairs, polarization_real, hamiltonian_real, preferred_element_type=jnp.float32
    ) + jnp.einsum(pairs, polarization_imag, hamiltonian_imag, preferred_element_type=jnp.float32)
    phonon_propagator_imag = jnp.einsum(
        pairs, polarization_imag, hamiltonian_real, preferred_element_type=jnp.float32
    ) - jnp.einsum(pairs, polarization_real, hamiltonian_imag, preferred_element_type=jnp.float32)
    live = (jnp.arange(tiles, dtype=jnp.int32)[None, :] < counts[:, None]).astype(jnp.float32)[
        :, :, None, None
    ]
    return jnp.stack([phonon_propagator_real * live, phonon_propagator_imag * live], axis=1).astype(
        jnp.bfloat16
    )


def body(green, contact, tile_count, offsets, pair_index, coupling_table):
    energies = green.shape[0]
    modes = offsets.shape[0]
    coupling = couplings(pair_index, coupling_table, coupling_table.shape[1])
    sigma = contact
    lesser = contact
    for sweep in range(ITERS):
        lesser = lesser_onsite(green[:, 0], sigma[:, 0], tile_count)[:, None]
        total = contact.astype(jnp.float32)
        padded = padded_2(lesser, (("energy", 0),), OMAX)
        banded_coupling = lax.all_to_all(
            padded, "momentum", split_axis=4, concat_axis=1, tiled=True
        )
        widened = banded_coupling.astype(jnp.float32)
        band_sum = jnp.zeros((energies,) + widened.shape[1:], jnp.float32)
        for phonon_mode in range(modes):
            mixed = jnp.einsum(
                "kq,eqabcd->ekabcd", coupling[phonon_mode], widened, precision=lax.Precision.HIGHEST
            )
            shift = offsets[phonon_mode]
            lower = lax.dynamic_slice_in_dim(mixed, OMAX - shift, energies, 0)
            upper = lax.dynamic_slice_in_dim(mixed, OMAX + shift, energies, 0)
            band_sum = band_sum + (lower + upper)
        phonon = lax.all_to_all(band_sum, "momentum", split_axis=1, concat_axis=4, tiled=True)
        total = total + phonon
        sigma = total.astype(jnp.bfloat16)
    return (lesser, sigma)


def solution(mesh):
    in_specs = (
        P("energy", "momentum", None, None, None),
        P("energy", "momentum", None, None, None, None),
        P("energy"),
        P(),
        P(),
        P(),
    )
    out_specs = (
        P("energy", "momentum", None, None, None, None),
        P("energy", "momentum", None, None, None, None),
    )
    return jax.shard_map(body, mesh=mesh, in_specs=in_specs, out_specs=out_specs, check_vma=False)
```

profile of v0, /device:TPU:928, one launch (start us, length us, event | category | flops | bytes accessed | tf_op | source)
XLA Modules:
  0.0 220.1 jit_solution(1944837199578791634)
XLA Ops:
  0.6 2.8 %copy.108 = bf16[3,1,2,384,384]{3,4,0,2,1:T(8,128)(2,1)S(1)} copy(bf16[3,1,2,384,384]{4,3,2,1,0:T(8,128)(2,1)} %param.6) | data formatting | bytes 3538944 | tf_op args[0]
  3.6 1.4 copy.106
  5.0 2.4 %copy.112 = bf16[3,1,384,384]{3,2,0,1:T(8,128)(2,1)S(1)} copy(bf16[3,1,384,384]{2,3,0,1:T(8,128)(2,1)S(1)} %get-tuple-element.13) | data formatting | bytes 1769472 | tf_op jit(solution)/shard_map/slice | solution.py:31
  7.4 1.6 fusion.38
  9.0 1.6 fusion.39
  10.6 2.3 %copy.116 = bf16[3,1,384,384]{3,2,0,1:T(8,128)(2,1)S(1)} copy(bf16[3,1,384,384]{2,3,0,1:T(8,128)(2,1)S(1)} %get-tuple-element.12) | data formatting | bytes 1769472 | tf_op jit(solution)/shard_map/slice | solution.py:32
  13.0 3.2 %fusion.18 = bf16[3,384,3,128]{1,3,2,0:T(8,128)(2,1)} fusion(f32[3,3,128,384]{3,2,1,0:T(8,128)} %fusion.38, bf16[3,384,3,128]{1,3,2,0:T(8,128)(2,1)S(1)} %bitcast.162, bf16[3,2,3,128,128]{3,4,2,0,1:T(8,128)(2,1)} %bitcast.182), kind=kOutput, calls=%fused_computation.26 | convolution fusion | flops 114130944 | bytes 3833856 | tf_op jit(solution)/shard_map/ertc,etcd->ertd/dot_general | solution.py:38
  16.2 3.4 %reshape.138 = bf16[3,3,128,384]{2,1,3,0:T(4,128)(2,1)} reshape(bf16[3,384,3,128]{1,3,2,0:T(8,128)(2,1)} %fusion.18) | data formatting | bytes 1769472 | tf_op jit(solution)/shard_map/reshape | solution.py:42
  19.6 3.3 %copy.150 = bf16[3,3,128,384]{3,2,1,0:T(8,128)(2,1)} copy(bf16[3,3,128,384]{2,1,3,0:T(4,128)(2,1)} %reshape.138) | data formatting | bytes 1769472 | tf_op jit(solution)/shard_map/reshape | solution.py:42
  22.9 2.9 %fusion.19 = bf16[3,384,3,128]{1,3,2,0:T(8,128)(2,1)} fusion(f32[3,3,128,384]{3,2,1,0:T(8,128)} %fusion.39, bf16[3,384,3,128]{1,3,2,0:T(8,128)(2,1)S(1)} %bitcast.163, bf16[3,2,3,128,128]{3,4,2,0,1:T(8,128)(2,1)} %bitcast.183), kind=kOutput, calls=%fused_computation.27 | convolution fusion | flops 114130944 | bytes 3833856 | tf_op jit(solution)/shard_map/ertc,etcd->ertd/dot_general | solution.py:41
  25.8 3.4 %reshape.139 = bf16[3,3,128,384]{2,1,3,0:T(4,128)(2,1)} reshape(bf16[3,384,3,128]{1,3,2,0:T(8,128)(2,1)} %fusion.19) | data formatting | bytes 1769472 | tf_op jit(solution)/shard_map/reshape | solution.py:45
  29.2 3.2 %copy.151 = bf16[3,3,128,384]{3,2,1,0:T(8,128)(2,1)} copy(bf16[3,3,128,384]{2,1,3,0:T(4,128)(2,1)} %reshape.139) | data formatting | bytes 1769472 | tf_op jit(solution)/shard_map/reshape | solution.py:45
  32.5 1.7 fusion.47
  36.5 1.9 collective-permute-start
  38.5 3.6 %collective-permute-start.1 = (bf16[3,1,2,3,128,128]{5,4,3,0,2,1:T(8,128)(2,1)S(1)}, bf16[3,1,2,3,128,128]{5,4,3,0,2,1:T(8,128)(2,1)S(1)}, u32[]{:S(2)}, u32[]{:S(2)}) collective-permute-start(bf16[3,1,2,3,128,128]{5,4,3,0,2,1:T(8,128)(2,1)S(1)} %pad_maximum_fusion.2), channel_id=1, source_target_pairs={{16,0},{32,16},{48,32},{64,48},{80,64},{96,80},{112,96},{128,112},... | collective-permute-start | bytes 1769480 | tf_op jit(solution)/shard_map/ppermute | solution.py:18
  42.1 5.6 %collective-permute-done = bf16[3,1,2,3,128,128]{5,4,3,0,2,1:T(8,128)(2,1)S(1)} collective-permute-done((bf16[3,1,2,3,128,128]{5,4,3,0,2,1:T(8,128)(2,1)S(1)}, bf16[3,1,2,3,128,128]{5,4,3,0,2,1:T(8,128)(2,1)S(1)}, u32[]{:S(2)}, u32[]{:S(2)}) %collective-permute-start) | collective-permute-done | bytes 589856 | tf_op jit(solution)/shard_map/ppermute | solution.py:15
  47.7 1.8 collective-permute-done.1
  49.7 3.1 %copy.117 = bf16[9,1,2,3,128,128]{5,2,3,1,0,4:T(2,128)(2,1)} copy(bf16[9,1,2,3,128,128]{5,4,3,0,2,1:T(8,128)(2,1)S(1)} %pad_maximum_fusion) | data formatting | bytes 3538944 | tf_op jit(solution)/shard_map/concatenate | solution.py:19
  52.8 7.2 %all-to-all-start = ((bf16[9,1,2,3,128,128]{5,2,3,1,0,4:T(2,128)(2,1)}), bf16[9,1,2,3,128,128]{5,2,3,1,0,4:T(2,128)(2,1)S(1)}, u32[]{:S(2)}, u32[]{:S(2)}) async-start(bf16[9,1,2,3,128,128]{5,2,3,1,0,4:T(2,128)(2,1)} %copy.117), calls=%async_computation | async-start | bytes 3538944 | tf_op jit(solution)/shard_map/all_to_all | solution.py:75
  68.2 2.9 %fusion.37 = f32[3,1,16,16]{3,1,2,0:T(1,128)} fusion(s32[3,16,16]{2,1,0:T(8,128)} %param.10, f32[3,16,1,1]{1,0,2,3:T(4,128)S(1)} %bitcast.157), kind=kOutput, calls=%fused_computation.56 | convolution fusion | flops 159744 | bytes 6336 | tf_op jit(solution)/shard_map/mkqc,mc->mkq/dot_general | solution.py:25
  71.1 19.6 %all-to-all-done = bf16[9,1,2,3,128,128]{5,2,3,1,0,4:T(2,128)(2,1)S(1)} async-done(((bf16[9,1,2,3,128,128]{5,2,3,1,0,4:T(2,128)(2,1)}), bf16[9,1,2,3,128,128]{5,2,3,1,0,4:T(2,128)(2,1)S(1)}, u32[]{:S(2)}, u32[]{:S(2)}) %all-to-all-start) | async-done | bytes 1769504 | tf_op jit(solution)/shard_map/all_to_all | solution.py:75
  90.7 2.4 %fusion.10 = f32[9,2,3,8,128,16]{4,5,3,2,1,0:T(8,128)S(1)} fusion(bf16[9,1,2,3,16,8,128]{6,2,3,0,5,4,1:T(2,128)(2,1)S(1)} %bitcast.166, f32[3,16,16]{2,1,0:T(8,128)} %bitcast.187), kind=kOutput, calls=%fused_computation.12 | convolution fusion | flops 169869312 | bytes 5316608 | tf_op jit(solution)/shard_map/kq,eqabcd->ekabcd/dot_general | solution.py:81
  93.0 1.6 fusion.6
  94.6 1.6 fusion.8
  97.3 22.3 %all_to_all.72 = f32[3,16,2,3,8,128]{5,4,3,2,0,1:T(8,128)S(1)} all-to-all(f32[3,16,2,3,8,128]{5,4,3,2,0,1:T(8,128)S(1)} %copy.120), channel_id=1, replica_groups=mesh['energy'=64,'momentum'=16] {'momentum'}, dimensions={1} | all-to-all | bytes 2359296 | tf_op jit(solution)/shard_map/all_to_all | solution.py:88
  119.8 1.4 copy.122
  121.2 1.4 fusion.36
  123.1 1.7 fusion.41
  125.2 1.7 reshape.140
  126.9 2.5 %copy.154 = bf16[3,3,128,384]{3,2,1,0:T(8,128)(2,1)S(1)} copy(bf16[3,3,128,384]{2,1,3,0:T(4,128)(2,1)} %reshape.140) | data formatting | bytes 1769472 | tf_op jit(solution)/shard_map/reshape | solution.py:42
  129.4 1.3 fusion.49
  131.2 1.3 fusion.21
  132.5 3.4 %reshape.141 = bf16[3,3,128,384]{2,1,3,0:T(4,128)(2,1)} reshape(bf16[3,384,3,128]{1,3,2,0:T(8,128)(2,1)} %fusion.21) | data formatting | bytes 1769472 | tf_op jit(solution)/shard_map/reshape | solution.py:45
  135.9 3.3 %copy.155 = bf16[3,3,128,384]{3,2,1,0:T(8,128)(2,1)} copy(bf16[3,3,128,384]{2,1,3,0:T(4,128)(2,1)} %reshape.141) | data formatting | bytes 1769472 | tf_op jit(solution)/shard_map/reshape | solution.py:45
  139.3 1.8 fusion.50
  142.2 1.9 collective-permute-start.2
  144.1 3.9 %collective-permute-start.3 = (bf16[3,1,2,3,128,128]{5,4,3,0,2,1:T(8,128)(2,1)S(1)}, bf16[3,1,2,3,128,128]{5,4,3,0,2,1:T(8,128)(2,1)S(1)}, u32[]{:S(2)}, u32[]{:S(2)}) collective-permute-start(bf16[3,1,2,3,128,128]{5,4,3,0,2,1:T(8,128)(2,1)S(1)} %pad_maximum_fusion.3), channel_id=1, source_target_pairs={{16,0},{32,16},{48,32},{64,48},{80,64},{96,80},{112,96},{128,112},... | collective-permute-start | bytes 1769480 | tf_op jit(solution)/shard_map/ppermute | solution.py:18
  148.0 5.4 %collective-permute-done.2 = bf16[3,1,2,3,128,128]{5,4,3,0,2,1:T(8,128)(2,1)S(1)} collective-permute-done((bf16[3,1,2,3,128,128]{5,4,3,0,2,1:T(8,128)(2,1)S(1)}, bf16[3,1,2,3,128,128]{5,4,3,0,2,1:T(8,128)(2,1)S(1)}, u32[]{:S(2)}, u32[]{:S(2)}) %collective-permute-start.2) | collective-permute-done | bytes 589856 | tf_op jit(solution)/shard_map/ppermute | solution.py:15
  153.4 1.8 collective-permute-done.3
  155.4 1.8 copy.129
  157.2 30.4 %all_to_all.73 = bf16[9,1,2,3,128,128]{5,2,3,1,0,4:T(2,128)(2,1)S(1)} all-to-all(bf16[9,1,2,3,128,128]{5,2,3,1,0,4:T(2,128)(2,1)S(1)} %copy.129), channel_id=1, replica_groups=mesh['energy'=64,'momentum'=16] {'momentum'}, dimensions={4} | all-to-all | bytes 3538944 | tf_op jit(solution)/shard_map/all_to_all | solution.py:75
  187.6 1.6 fusion.2
  189.2 1.6 fusion.4
  190.7 1.6 fusion
  193.0 1.4 copy.132
  194.4 3.7 %all-to-all-start.3 = ((f32[3,16,2,3,8,128]{5,4,3,2,0,1:T(8,128)}), f32[3,16,2,3,8,128]{5,4,3,2,0,1:T(8,128)S(1)}, u32[]{:S(2)}, u32[]{:S(2)}) async-start(f32[3,16,2,3,8,128]{5,4,3,2,0,1:T(8,128)} %copy.132), calls=%async_computation.3 | async-start | bytes 2359296 | tf_op jit(solution)/shard_map/all_to_all | solution.py:88
  199.0 19.4 %all-to-all-done.3 = f32[3,16,2,3,8,128]{5,4,3,2,0,1:T(8,128)S(1)} async-done(((f32[3,16,2,3,8,128]{5,4,3,2,0,1:T(8,128)}), f32[3,16,2,3,8,128]{5,4,3,2,0,1:T(8,128)S(1)}, u32[]{:S(2)}, u32[]{:S(2)}) %all-to-all-start.3) | async-done | bytes 1179680 | tf_op jit(solution)/shard_map/all_to_all | solution.py:88
  219.1 1.1 copy.136
  (60 shorter events, 9.3 us)
Async XLA Ops:
  0.6 67.5 %copy-start = (f32[3,16]{1,0:T(4,128)S(1)}, f32[3,16]{1,0:T(4,128)}, u32[]{:S(2)}) copy-start(f32[3,16]{1,0:T(4,128)} %param.11) | copy-start | bytes 580
  5.0 4.0 %copy-start.6 = (bf16[3,1,2,3,128,128]{4,5,3,0,2,1:T(8,128)(2,1)}, bf16[3,1,2,3,128,128]{4,5,3,0,2,1:T(8,128)(2,1)S(1)}, u32[]{:S(2)}) copy-start(bf16[3,1,2,3,128,128]{4,5,3,0,2,1:T(8,128)(2,1)S(1)} %copy.106) | copy-start | bytes 1769476
  7.4 26.9 %copy-start.4 = (bf16[3,1,384,384]{3,2,0,1:T(8,128)(2,1)}, bf16[3,1,384,384]{3,2,0,1:T(8,128)(2,1)S(1)}, u32[]{:S(2)}) copy-start(bf16[3,1,384,384]{3,2,0,1:T(8,128)(2,1)S(1)} %copy.112) | copy-start | bytes 2654212
  13.0 22.4 %copy-start.2 = (bf16[3,1,384,384]{3,2,0,1:T(8,128)(2,1)}, bf16[3,1,384,384]{3,2,0,1:T(8,128)(2,1)S(1)}, u32[]{:S(2)}) copy-start(bf16[3,1,384,384]{3,2,0,1:T(8,128)(2,1)S(1)} %copy.116) | copy-start | bytes 2654212
  25.8 6.7 %copy-start.18 = (s32[3]{0:T(128)S(1)}, s32[3]{0:T(128)}, u32[]{:S(2)}) copy-start(s32[3]{0:T(128)} %param.8) | copy-start | bytes 40
  32.4 1.8 copy-start.9
  34.8 1.2 copy-start.8
  36.5 11.2 %collective-permute-start = (bf16[3,1,2,3,128,128]{5,4,3,0,2,1:T(8,128)(2,1)S(1)}, bf16[3,1,2,3,128,128]{5,4,3,0,2,1:T(8,128)(2,1)S(1)}, u32[]{:S(2)}, u32[]{:S(2)}) collective-permute-start(bf16[3,1,2,3,128,128]{5,4,3,0,2,1:T(8,128)(2,1)S(1)} %pad_maximum_fusion.2), channel_id=1, source_target_pairs={{0,16},{16,32},{32,48},{48,64},{64,80},{80,96},{96,112},{112,128},... | collective-permute-start | bytes 1769480 | tf_op jit(solution)/shard_map/ppermute | solution.py:15
  38.5 11.0 %collective-permute-start.1 = (bf16[3,1,2,3,128,128]{5,4,3,0,2,1:T(8,128)(2,1)S(1)}, bf16[3,1,2,3,128,128]{5,4,3,0,2,1:T(8,128)(2,1)S(1)}, u32[]{:S(2)}, u32[]{:S(2)}) collective-permute-start(bf16[3,1,2,3,128,128]{5,4,3,0,2,1:T(8,128)(2,1)S(1)} %pad_maximum_fusion.2), channel_id=1, source_target_pairs={{16,0},{32,16},{48,32},{64,48},{80,64},{96,80},{112,96},{128,112},... | collective-permute-start | bytes 1769480 | tf_op jit(solution)/shard_map/ppermute | solution.py:18
  52.8 7.2 %copy-start.17 = (s32[3]{0:T(128)S(1)}, s32[3]{0:T(128)}, u32[]{:S(2)}) copy-start(s32[3]{0:T(128)} %param.9) | copy-start | bytes 40
  52.8 37.9 %all-to-all-start = ((bf16[9,1,2,3,128,128]{5,2,3,1,0,4:T(2,128)(2,1)}), bf16[9,1,2,3,128,128]{5,2,3,1,0,4:T(2,128)(2,1)S(1)}, u32[]{:S(2)}, u32[]{:S(2)}) async-start(bf16[9,1,2,3,128,128]{5,2,3,1,0,4:T(2,128)(2,1)} %copy.117), calls=%async_computation | async-start | bytes 3538944 | tf_op jit(solution)/shard_map/all_to_all | solution.py:75
  90.7 2.4 %copy-start.15 = (f32[3,1,16,16]{3,1,2,0:T(1,128)S(1)}, f32[3,1,16,16]{3,1,2,0:T(1,128)}, u32[]{:S(2)}) copy-start(f32[3,1,16,16]{3,1,2,0:T(1,128)} %fusion.37) | copy-start | bytes 9220
  119.8 1.4 copy-start.7
  122.7 2.1 copy-start.12
  125.2 4.2 %copy-start.5 = (bf16[3,1,384,384]{3,2,0,1:T(8,128)(2,1)S(1)}, bf16[3,1,384,384]{3,2,0,1:T(8,128)(2,1)}, u32[]{:S(2)}) copy-start(bf16[3,1,384,384]{3,2,0,1:T(8,128)(2,1)} %copy-done.4) | copy-start | bytes 2654212
  129.4 1.5 copy-start.11
  129.4 1.8 copy-start.13
  135.9 5.1 %copy-start.3 = (bf16[3,1,384,384]{3,2,0,1:T(8,128)(2,1)S(1)}, bf16[3,1,384,384]{3,2,0,1:T(8,128)(2,1)}, u32[]{:S(2)}) copy-start(bf16[3,1,384,384]{3,2,0,1:T(8,128)(2,1)} %copy-done.2) | copy-start | bytes 2654212
  139.3 1.8 copy-start.10
  139.3 1.8 copy-start.14
  142.2 11.2 %collective-permute-start.2 = (bf16[3,1,2,3,128,128]{5,4,3,0,2,1:T(8,128)(2,1)S(1)}, bf16[3,1,2,3,128,128]{5,4,3,0,2,1:T(8,128)(2,1)S(1)}, u32[]{:S(2)}, u32[]{:S(2)}) collective-permute-start(bf16[3,1,2,3,128,128]{5,4,3,0,2,1:T(8,128)(2,1)S(1)} %pad_maximum_fusion.3), channel_id=1, source_target_pairs={{0,16},{16,32},{32,48},{48,64},{64,80},{80,96},{96,112},{112,128},... | collective-permute-start | bytes 1769480 | tf_op jit(solution)/shard_map/ppermute | solution.py:15
  144.1 11.0 %collective-permute-start.3 = (bf16[3,1,2,3,128,128]{5,4,3,0,2,1:T(8,128)(2,1)S(1)}, bf16[3,1,2,3,128,128]{5,4,3,0,2,1:T(8,128)(2,1)S(1)}, u32[]{:S(2)}, u32[]{:S(2)}) collective-permute-start(bf16[3,1,2,3,128,128]{5,4,3,0,2,1:T(8,128)(2,1)S(1)} %pad_maximum_fusion.3), channel_id=1, source_target_pairs={{16,0},{32,16},{48,32},{64,48},{80,64},{96,80},{112,96},{128,112},... | collective-permute-start | bytes 1769480 | tf_op jit(solution)/shard_map/ppermute | solution.py:18
  157.2 30.4 %copy-start.16 = (f32[3,1,16,16]{3,1,2,0:T(1,128)S(1)}, f32[3,1,16,16]{3,1,2,0:T(1,128)}, u32[]{:S(2)}) copy-start(f32[3,1,16,16]{3,1,2,0:T(1,128)} %fusion.37) | copy-start | bytes 9220
  194.4 24.0 %all-to-all-start.3 = ((f32[3,16,2,3,8,128]{5,4,3,2,0,1:T(8,128)}), f32[3,16,2,3,8,128]{5,4,3,2,0,1:T(8,128)S(1)}, u32[]{:S(2)}, u32[]{:S(2)}) async-start(f32[3,16,2,3,8,128]{5,4,3,2,0,1:T(8,128)} %copy.132), calls=%async_computation.3 | async-start | bytes 2359296 | tf_op jit(solution)/shard_map/all_to_all | solution.py:88
  218.5 1.6 copy-start.1
where the time goes:
time: 222 us; the launch traced here: 220 us
  waiting for transfers between devices  53.6 us (24%)
  blocking collectives  52.7 us (24%)
  local copies, waits for them, and re-layouts  45.8 us (21%)
  matrix products  33.7 us (15%)
  starting transfers between devices  22.2 us (10%)
  between operations  8.66 us (4%)
  other arithmetic  3.55 us (2%)
    all_to_all x1, blocking collectives, body(): lax.all_to_all(padded, 'momentum', split_axis=4, concat_axis=1, tiled=True)  30.4 us
    all_to_all x1, blocking collectives, body(): lax.all_to_all(band_sum, 'momentum', split_axis=1, concat_axis=4, tiled=T...  22.3 us
    all_to_all x1, waiting for transfers between devices, body(): lax.all_to_all(padded, 'momentum', split_axis=4, concat_axis=1, tiled=True)  19.6 us
    all_to_all x1, waiting for transfers between devices, body(): lax.all_to_all(band_sum, 'momentum', split_axis=1, concat_axis=4, tiled=T...  19.4 us
    reshape x4, local copies, waits for them, and re-layouts, lesser_onsite(): polarization_imag.astype(jnp.bfloat16)  13.4 us
    ppermute x2, waiting for transfers between devices, padded_2(): lax.ppermute(lax.slice_in_dim(block, block.shape[dim] - width, None, axis...  11 us
    reshape x4, local copies, waits for them, and re-layouts, lesser_onsite(): polarization_real.astype(jnp.bfloat16)  10.9 us
    dot_general x6, matrix products, body(): jnp.einsum('kq,eqabcd->ekabcd', coupling[phonon_mode], widened, precision...  10.3 us
  transfers between devices with their start and end apart: 6, of which 6 were waited for; matrix products, arithmetic and copies ran while one was open for 2% of the time, Pallas kernels for 0%

commit v1 on v0

v1 whole, which is shorter than its diff:
```python
import functools

import jax
import jax.numpy as jnp
from jax import lax
from jax.experimental import pallas as pl
from jax.experimental.pallas import tpu as pltpu
from jax.sharding import PartitionSpec as P

ITERS = 2
F32 = jnp.float32
BF16 = jnp.bfloat16
PARAMS = pltpu.CompilerParams(vmem_limit_bytes=12 << 20)
LESSER_COST = pl.CostEstimate(flops=900_000_000, bytes_accessed=4_000_000, transcendentals=0)


def coupling_kernel(span, odd, offsets, table, pairs, out):
    modes, momenta = pairs.shape[0], pairs.shape[1]
    window = 3 * span
    order = lax.broadcasted_iota(jnp.int32, (momenta, window * momenta), 0)
    column = lax.broadcasted_iota(jnp.int32, (momenta, window * momenta), 1)
    energy = lax.div(column, momenta)
    mirrored = energy + jnp.where(energy < span, 2 * span, jnp.where(energy < 2 * span, 0, -2 * span))
    energy = jnp.where(odd[0] == 1, mirrored, energy)
    spread = (lax.rem(column, momenta) == order).astype(F32)
    wide = []
    for m in range(modes):
        entry = pairs[m]
        value = jnp.zeros(entry.shape, F32)
        for c in range(table.shape[1]):
            value = jnp.where(entry == c, table[m, c], value)
        wide.append(jnp.dot(value, spread, precision=lax.Precision.HIGHEST, preferred_element_type=F32))
    for j in range(span):
        total = jnp.zeros(energy.shape, F32)
        for m in range(modes):
            low = (energy == j + span - offsets[m]).astype(F32)
            high = (energy == j + span + offsets[m]).astype(F32)
            total = total + wide[m] * (low + high)
        first = total.astype(BF16)
        out[pl.ds(j * momenta, momenta), :] = first
        out[pl.ds((span + j) * momenta, momenta), :] = (total - first.astype(F32)).astype(BF16)


def lesser_point(green, sigma, count):
    tiles, width = sigma.shape[1], sigma.shape[2]
    g_real, g_imag = green[0], green[1]
    cols = [slice(t * width, (t + 1) * width) for t in range(tiles)]
    product = []
    for t in range(tiles):
        left = jnp.concatenate([g_real[:, cols[t]], g_imag[:, cols[t]]], axis=1)
        s_real, s_imag = sigma[0, t], sigma[1, t]
        right = jnp.concatenate(
            [jnp.concatenate([s_real, s_imag], axis=1), jnp.concatenate([-s_imag, s_real], axis=1)], axis=0
        )
        product.append(jnp.dot(left, right, preferred_element_type=F32).astype(BF16))
    reals, imags = [], []
    for t in range(tiles):
        left = jnp.concatenate([product[u][cols[t]] for u in range(tiles)], axis=1)
        r = [g_real[cols[t], cols[u]] for u in range(tiles)]
        i = [g_imag[cols[t], cols[u]] for u in range(tiles)]
        top = jnp.concatenate([x for u in range(tiles) for x in (r[u], i[u])], axis=1)
        low = jnp.concatenate([x for u in range(tiles) for x in (-i[u], r[u])], axis=1)
        right = jnp.concatenate([top, low], axis=0)
        both = lax.dot_general(left, right, (((1,), (1,)), ((), ())), preferred_element_type=F32)
        live = jnp.where(t < count, 1.0, 0.0).astype(F32)
        both = (both * live).astype(BF16)
        reals.append(both[:, :width])
        imags.append(both[:, width:])
    return jnp.concatenate(reals + imags, axis=0)


def first_kernel(counts, green, contact, sent, blocks, tiles, live, sems):
    energies = green.shape[0]
    count_copy = pltpu.make_async_copy(counts, live, sems.at[2 * energies])
    copies = []
    for e in range(energies):
        copies.append(pltpu.make_async_copy(contact.at[e, 0], tiles.at[e], sems.at[2 * e]))
        copies.append(pltpu.make_async_copy(green.at[e, 0], blocks.at[e], sems.at[2 * e + 1]))
        copies[-2].start()
        copies[-1].start()
        if e == 0:
            count_copy.start()
    for e in range(energies):
        copies[2 * e].wait()
        copies[2 * e + 1].wait()
        if e == 0:
            count_copy.wait()
        flat = lesser_point(blocks[e], tiles[e], live[e])
        sent[:, e] = flat.reshape(sent.shape[0], sent.shape[2], sent.shape[3])


def next_kernel(counts, green, contact, phonon, sent, kept):
    for e in range(green.shape[0]):
        back = phonon[:, e].reshape(contact.shape[2:])
        sigma = (contact[e, 0].astype(F32) + back.astype(F32)).astype(BF16)
        flat = lesser_point(green[e, 0], sigma, counts[e])
        sent[:, e] = flat.reshape(sent.shape[0], sent.shape[2], sent.shape[3])
        kept[e, 0] = flat.reshape(kept.shape[2:])


def mix_kernel(span, matrix, across, own, beside, out, turned, mixed):
    momenta, rows = own.shape[0], own.shape[2]
    for part, source in enumerate((across, own, beside)):
        for i in range(span):
            at = (part * span + i) * momenta
            turned[:, at : at + momenta, :] = jnp.swapaxes(source[:, i], 0, 1)
    half = span * momenta
    for r in range(0, rows, 2):
        right = jnp.concatenate([turned[r], turned[r + 1]], axis=1)
        both = jnp.dot(matrix[...], right, preferred_element_type=F32)
        both = (both[:half] + both[half:]).astype(BF16)
        mixed[r] = both[:, : right.shape[1] // 2]
        mixed[r + 1] = both[:, right.shape[1] // 2 :]
    for j in range(span):
        out[:, j] = jnp.swapaxes(mixed[:, j * momenta : (j + 1) * momenta, :], 0, 1)


def total_kernel(contact, phonon, out):
    for e in range(contact.shape[0]):
        back = phonon[:, e].reshape(contact.shape[2:])
        out[e, 0] = (contact[e, 0].astype(F32) + back.astype(F32)).astype(BF16)


def couplings(span, odd, offsets, table, pairs):
    momenta = pairs.shape[1]
    smem = pl.BlockSpec(memory_space=pltpu.SMEM)
    vmem = pl.BlockSpec(memory_space=pltpu.VMEM)
    return pl.pallas_call(
        functools.partial(coupling_kernel, span),
        out_shape=jax.ShapeDtypeStruct((2 * span * momenta, 3 * span * momenta), BF16),
        in_specs=[smem, smem, smem, vmem],
        out_specs=vmem,
        name="couplings",
        compiler_params=PARAMS,
        cost_estimate=pl.CostEstimate(flops=200000, bytes_accessed=40000, transcendentals=0),
    )(odd, offsets, table, pairs)


def chunks_of(contact, momenta):
    energies, _, parts, tiles, width, _ = contact.shape
    return jax.ShapeDtypeStruct((momenta, energies, parts * tiles * width // momenta, width), BF16)


def first_lesser(counts, green, contact, momenta):
    hbm = pl.BlockSpec(memory_space=pltpu.HBM)
    energies = green.shape[0]
    return pl.pallas_call(
        first_kernel,
        out_shape=chunks_of(contact, momenta),
        in_specs=[hbm, hbm, hbm],
        out_specs=pl.BlockSpec(memory_space=pltpu.VMEM),
        scratch_shapes=[
            pltpu.VMEM((energies,) + green.shape[2:], BF16),
            pltpu.VMEM((energies,) + contact.shape[2:], BF16),
            pltpu.SMEM((energies,), jnp.int32),
            pltpu.SemaphoreType.DMA((2 * energies + 1,)),
        ],
        name="lesser_first",
        compiler_params=PARAMS,
        cost_estimate=LESSER_COST,
    )(counts, green, contact)


def next_lesser(counts, green, contact, phonon, momenta):
    vmem = pl.BlockSpec(memory_space=pltpu.VMEM)
    return pl.pallas_call(
        next_kernel,
        out_shape=(chunks_of(contact, momenta), jax.ShapeDtypeStruct(contact.shape, BF16)),
        in_specs=[pl.BlockSpec(memory_space=pltpu.SMEM), vmem, vmem, vmem],
        out_specs=(vmem, vmem),
        name="lesser_next",
        compiler_params=PARAMS,
        cost_estimate=LESSER_COST,
    )(counts, green, contact, phonon)


def mix(matrix, across, own, beside):
    momenta, span, rows, width = own.shape
    vmem = pl.BlockSpec(memory_space=pltpu.VMEM)
    return pl.pallas_call(
        functools.partial(mix_kernel, span),
        out_shape=jax.ShapeDtypeStruct(own.shape, BF16),
        in_specs=[vmem] * 4,
        out_specs=vmem,
        scratch_shapes=[
            pltpu.VMEM((rows, 3 * span * momenta, width), BF16),
            pltpu.VMEM((rows, span * momenta, width), BF16),
        ],
        name="mix",
        compiler_params=PARAMS,
        cost_estimate=pl.CostEstimate(flops=200_000_000, bytes_accessed=2_400_000, transcendentals=0),
    )(matrix, across, own, beside)


def total(contact, phonon):
    vmem = pl.BlockSpec(memory_space=pltpu.VMEM)
    return pl.pallas_call(
        total_kernel,
        out_shape=jax.ShapeDtypeStruct(contact.shape, BF16),
        in_specs=[vmem, vmem],
        out_specs=vmem,
        name="total",
        compiler_params=PARAMS,
    )(contact, phonon)


def exchange(block):
    return lax.all_to_all(block, "momentum", split_axis=0, concat_axis=0, tiled=True)


def body(green, contact, tile_count, offsets, pair_index, coupling_table):
    momenta = pair_index.shape[1]
    span = green.shape[0]
    count = lax.axis_size("energy")
    even = [(a, b) for i in range(0, count - 1, 2) for a, b in ((i, i + 1), (i + 1, i))]
    odd = [(a, b) for i in range(1, count - 1, 2) for a, b in ((i, i + 1), (i + 1, i))]
    parity = lax.rem(lax.axis_index("energy"), 2).astype(jnp.int32).reshape(1)
    matrix = couplings(span, parity, offsets, coupling_table, pair_index)
    held = [pltpu.with_memory_space_constraint(x, pltpu.HBM) for x in (tile_count, green, contact)]
    sent = first_lesser(*held, momenta)
    for sweep in range(ITERS):
        if sweep > 0:
            sent, kept = next_lesser(tile_count, green, contact, phonon, momenta)
        own = exchange(sent)
        across = lax.ppermute(own, "energy", odd)
        beside = lax.ppermute(own, "energy", even)
        phonon = exchange(mix(matrix, across, own, beside))
    return kept, total(contact, phonon)


def solution(mesh):
    in_specs = (
        P("energy", "momentum", None, None, None),
        P("energy", "momentum", None, None, None, None),
        P("energy"),
        P(),
        P(),
        P(),
    )
    out_specs = (
        P("energy", "momentum", None, None, None, None),
        P("energy", "momentum", None, None, None, None),
    )
    return jax.shard_map(body, mesh=mesh, in_specs=in_specs, out_specs=out_specs, check_vma=False)
```

time: 222 us -> 105 us (0.47)
  the two profiles are of different devices: /device:TPU:928 before, /device:TPU:481 now
where the time goes in v1:
time: 105 us
  blocking collectives  62.1 us (59%)
  waiting for transfers between devices  16.5 us (16%)
  starting transfers between devices  14.8 us (14%)
  Pallas kernels  10.6 us (10%)
    all_to_all x4, blocking collectives, exchange(): lax.all_to_all(block, 'momentum', split_axis=0, concat_axis=0, tiled=True)  62.1 us
    ppermute x2, waiting for transfers between devices, body(): across = lax.ppermute(own, 'energy', odd)  16.5 us
    ppermute x2, starting transfers between devices, body(): across = lax.ppermute(own, 'energy', odd)  7.42 us
    ppermute x2, starting transfers between devices, body(): beside = lax.ppermute(own, 'energy', even)  7.4 us
    pallas_call x1, Pallas kernels, first_lesser(): pl.pallas_call(first_kernel, out_shape=chunks_of(contact, momenta), in_sp...  3.43 us
    pallas_call x1, Pallas kernels, next_lesser(): pl.pallas_call(next_kernel, out_shape=(chunks_of(contact, momenta), jax.S...  3.05 us
    pallas_call x2, Pallas kernels, mix(): pl.pallas_call(functools.partial(mix_kernel, span), out_shape=jax.ShapeDt...  2.34 us
  transfers between devices with their start and end apart: 4, of which 2 were waited for; matrix products, arithmetic and copies ran while one was open for 0% of the time, Pallas kernels for 1%

profile of v1, /device:TPU:481, one launch (start us, length us, event | category | flops | bytes accessed | tf_op | source)
XLA Modules:
  0.0 104.8 jit_solution(13561271232016448804)
XLA Ops:
  0.6 0.0 copy-start.2
  0.6 0.0 copy-start.1
  0.7 0.0 copy-start.3
  0.7 3.4 %lesser_first.1 = bf16[16,3,48,128]{3,2,1,0:T(8,128)(2,1)S(1)} custom-call(s32[3]{0:T(128)} %counts.3, bf16[3,1,2,384,384]{4,3,2,1,0:T(8,128)(2,1)} %green.3, bf16[3,1,2,3,128,128]{5,4,3,2,1,0:T(8,128)(2,1)} %contact.5), custom_call_target="tpu_custom_call" | custom-call | flops 900000000 | bytes 4000000 | tf_op jit(solution)/shard_map/lesser_first/pallas_call | solution.py:147
  4.1 17.9 %all_to_all.20.own = bf16[16,3,48,128]{3,2,1,0:T(8,128)(2,1)S(1)} all-to-all(bf16[16,3,48,128]{3,2,1,0:T(8,128)(2,1)S(1)} %lesser_first.1), channel_id=1, replica_groups=mesh['energy'=64,'momentum'=16] {'momentum'}, dimensions={0} | all-to-all | bytes 1179648 | tf_op jit(solution)/shard_map/all_to_all | solution.py:208
  22.0 3.8 %collective-permute-start.1 = (bf16[16,3,48,128]{3,2,1,0:T(8,128)(2,1)S(1)}, bf16[16,3,48,128]{3,2,1,0:T(8,128)(2,1)S(1)}, u32[]{:S(2)}, u32[]{:S(2)}) collective-permute-start(bf16[16,3,48,128]{3,2,1,0:T(8,128)(2,1)S(1)} %all_to_all.20.own), channel_id=1, source_target_pairs={{0,16},{16,0},{32,48},{48,32},{64,80},{80,64},{96,112},{112,96},{1... | collective-permute-start | bytes 1769480 | tf_op jit(solution)/shard_map/ppermute | solution.py:226
  25.8 4.7 %collective-permute-start = (bf16[16,3,48,128]{3,2,1,0:T(8,128)(2,1)S(1)}, bf16[16,3,48,128]{3,2,1,0:T(8,128)(2,1)S(1)}, u32[]{:S(2)}, u32[]{:S(2)}) collective-permute-start(bf16[16,3,48,128]{3,2,1,0:T(8,128)(2,1)S(1)} %all_to_all.20.own), channel_id=1, source_target_pairs={{16,32},{32,16},{48,64},{64,48},{80,96},{96,80},{112,128},{128,112... | collective-permute-start | bytes 1769480 | tf_op jit(solution)/shard_map/ppermute | solution.py:225
  30.4 0.0 copy-done.2
  30.5 0.0 copy-done.1
  30.5 0.0 copy-done.3
  30.5 0.8 couplings.1.matrix
  31.3 0.0 copy-start
  31.3 0.0 copy-start.4
  31.3 0.0 copy-start.5
  31.3 0.0 collective-permute-done.1.beside
  31.3 6.9 %collective-permute-done.across = bf16[16,3,48,128]{3,2,1,0:T(8,128)(2,1)S(1)} collective-permute-done((bf16[16,3,48,128]{3,2,1,0:T(8,128)(2,1)S(1)}, bf16[16,3,48,128]{3,2,1,0:T(8,128)(2,1)S(1)}, u32[]{:S(2)}, u32[]{:S(2)}) %collective-permute-start) | collective-permute-done | bytes 589856 | tf_op jit(solution)/shard_map/ppermute | solution.py:225
  38.2 1.2 %mix.2 = bf16[16,3,48,128]{3,2,1,0:T(8,128)(2,1)S(1)} custom-call(bf16[96,144]{1,0:T(8,128)(2,1)S(1)} %couplings.1.matrix, bf16[16,3,48,128]{3,2,1,0:T(8,128)(2,1)S(1)} %collective-permute-done.across, bf16[16,3,48,128]{3,2,1,0:T(8,128)(2,1)S(1)} %all_to_all.20.own, bf16[16,3,48,128]{3,2,1,0:T(8,128)(2,1)S(1)} %collective-permute-done.1.beside), custom_call_target="tpu_custom_call" | custom-call | flops 200000000 | bytes 2400000 | tf_op jit(solution)/shard_map/mix/pallas_call | solution.py:180
  39.4 14.9 %all_to_all.21.phonon = bf16[16,3,48,128]{3,2,1,0:T(8,128)(2,1)S(1)} all-to-all(bf16[16,3,48,128]{3,2,1,0:T(8,128)(2,1)S(1)} %mix.2), channel_id=1, replica_groups=mesh['energy'=64,'momentum'=16] {'momentum'}, dimensions={0} | all-to-all | bytes 1179648 | tf_op jit(solution)/shard_map/all_to_all | solution.py:208
  54.3 0.0 copy-done
  54.3 0.0 copy-done.4
  54.3 0.0 copy-done.5
  54.3 3.0 %lesser_next.1 = (bf16[16,3,48,128]{3,2,1,0:T(8,128)(2,1)S(1)}, bf16[3,1,2,3,128,128]{5,4,3,2,1,0:T(8,128)(2,1)}) custom-call(s32[3]{0:T(128)S(1)} %copy-done.5, bf16[3,1,2,384,384]{4,3,2,1,0:T(8,128)(2,1)S(1)} %copy-done.4, bf16[3,1,2,3,128,128]{5,4,3,2,1,0:T(8,128)(2,1)S(1)} %copy-done, bf16[16,3,48,128]{3,2,1,0:T(8,128)(2,1)S(1)} %all_to_all.21.phonon), custom_call_target="tpu_custom_call" | custom-call | flops 900000000 | bytes 4000000 | tf_op jit(solution)/shard_map/lesser_next/pallas_call | solution.py:166
  57.4 14.4 %all_to_all.22.own = bf16[16,3,48,128]{3,2,1,0:T(8,128)(2,1)S(1)} all-to-all(bf16[16,3,48,128]{3,2,1,0:T(8,128)(2,1)S(1)} %get-tuple-element.5), channel_id=1, replica_groups=mesh['energy'=64,'momentum'=16] {'momentum'}, dimensions={0} | all-to-all | bytes 1179648 | tf_op jit(solution)/shard_map/all_to_all | solution.py:208
  71.7 3.6 %collective-permute-start.3 = (bf16[16,3,48,128]{3,2,1,0:T(8,128)(2,1)S(1)}, bf16[16,3,48,128]{3,2,1,0:T(8,128)(2,1)S(1)}, u32[]{:S(2)}, u32[]{:S(2)}) collective-permute-start(bf16[16,3,48,128]{3,2,1,0:T(8,128)(2,1)S(1)} %all_to_all.22.own), channel_id=1, source_target_pairs={{0,16},{16,0},{32,48},{48,32},{64,80},{80,64},{96,112},{112,96},{1... | collective-permute-start | bytes 1769480 | tf_op jit(solution)/shard_map/ppermute | solution.py:226
  75.3 2.8 %collective-permute-start.2 = (bf16[16,3,48,128]{3,2,1,0:T(8,128)(2,1)S(1)}, bf16[16,3,48,128]{3,2,1,0:T(8,128)(2,1)S(1)}, u32[]{:S(2)}, u32[]{:S(2)}) collective-permute-start(bf16[16,3,48,128]{3,2,1,0:T(8,128)(2,1)S(1)} %all_to_all.22.own), channel_id=1, source_target_pairs={{16,32},{32,16},{48,64},{64,48},{80,96},{96,80},{112,128},{128,112... | collective-permute-start | bytes 1769480 | tf_op jit(solution)/shard_map/ppermute | solution.py:225
  78.1 0.0 collective-permute-done.3.beside
  78.1 9.6 %collective-permute-done.2.across = bf16[16,3,48,128]{3,2,1,0:T(8,128)(2,1)S(1)} collective-permute-done((bf16[16,3,48,128]{3,2,1,0:T(8,128)(2,1)S(1)}, bf16[16,3,48,128]{3,2,1,0:T(8,128)(2,1)S(1)}, u32[]{:S(2)}, u32[]{:S(2)}) %collective-permute-start.2) | collective-permute-done | bytes 589856 | tf_op jit(solution)/shard_map/ppermute | solution.py:225
  87.7 1.2 %mix.3 = bf16[16,3,48,128]{3,2,1,0:T(8,128)(2,1)S(1)} custom-call(bf16[96,144]{1,0:T(8,128)(2,1)S(1)} %couplings.1.matrix, bf16[16,3,48,128]{3,2,1,0:T(8,128)(2,1)S(1)} %collective-permute-done.2.across, bf16[16,3,48,128]{3,2,1,0:T(8,128)(2,1)S(1)} %all_to_all.22.own, bf16[16,3,48,128]{3,2,1,0:T(8,128)(2,1)S(1)} %collective-permute-done.3.beside), custom_call_target="tpu_custom_call" | custom-call | flops 200000000 | bytes 2400000 | tf_op jit(solution)/shard_map/mix/pallas_call | solution.py:180
  88.9 14.9 %all_to_all.23.phonon = bf16[16,3,48,128]{3,2,1,0:T(8,128)(2,1)S(1)} all-to-all(bf16[16,3,48,128]{3,2,1,0:T(8,128)(2,1)S(1)} %mix.3), channel_id=1, replica_groups=mesh['energy'=64,'momentum'=16] {'momentum'}, dimensions={0} | all-to-all | bytes 1179648 | tf_op jit(solution)/shard_map/all_to_all | solution.py:208
  103.8 1.0 total.1
Async XLA Ops:
  0.6 29.8 %copy-start.2 = (f32[3,16]{1,0:T(4,128)S(1)}, f32[3,16]{1,0:T(4,128)}, u32[]{:S(2)}) copy-start(f32[3,16]{1,0:T(4,128)} %table.1) | copy-start | bytes 580
  0.6 29.8 %copy-start.1 = (s32[3,16,16]{2,1,0:T(8,128)S(1)}, s32[3,16,16]{2,1,0:T(8,128)}, u32[]{:S(2)}) copy-start(s32[3,16,16]{2,1,0:T(8,128)} %pairs.1) | copy-start | bytes 9220
  0.7 29.8 %copy-start.3 = (s32[3]{0:T(128)S(1)}, s32[3]{0:T(128)}, u32[]{:S(2)}) copy-start(s32[3]{0:T(128)} %offsets.1) | copy-start | bytes 40
  22.0 9.3 %collective-permute-start.1 = (bf16[16,3,48,128]{3,2,1,0:T(8,128)(2,1)S(1)}, bf16[16,3,48,128]{3,2,1,0:T(8,128)(2,1)S(1)}, u32[]{:S(2)}, u32[]{:S(2)}) collective-permute-start(bf16[16,3,48,128]{3,2,1,0:T(8,128)(2,1)S(1)} %all_to_all.20.own), channel_id=1, source_target_pairs={{0,16},{16,0},{32,48},{48,32},{64,80},{80,64},{96,112},{112,96},{1... | collective-permute-start | bytes 1769480 | tf_op jit(solution)/shard_map/ppermute | solution.py:226
  25.8 12.4 %collective-permute-start = (bf16[16,3,48,128]{3,2,1,0:T(8,128)(2,1)S(1)}, bf16[16,3,48,128]{3,2,1,0:T(8,128)(2,1)S(1)}, u32[]{:S(2)}, u32[]{:S(2)}) collective-permute-start(bf16[16,3,48,128]{3,2,1,0:T(8,128)(2,1)S(1)} %all_to_all.20.own), channel_id=1, source_target_pairs={{16,32},{32,16},{48,64},{64,48},{80,96},{96,80},{112,128},{128,112... | collective-permute-start | bytes 1769480 | tf_op jit(solution)/shard_map/ppermute | solution.py:225
  31.3 23.0 %copy-start = (bf16[3,1,2,3,128,128]{5,4,3,2,1,0:T(8,128)(2,1)S(1)}, bf16[3,1,2,3,128,128]{5,4,3,2,1,0:T(8,128)(2,1)}, u32[]{:S(2)}) copy-start(bf16[3,1,2,3,128,128]{5,4,3,2,1,0:T(8,128)(2,1)} %contact.5) | copy-start | bytes 1769476
  31.3 23.0 %copy-start.4 = (bf16[3,1,2,384,384]{4,3,2,1,0:T(8,128)(2,1)S(1)}, bf16[3,1,2,384,384]{4,3,2,1,0:T(8,128)(2,1)}, u32[]{:S(2)}) copy-start(bf16[3,1,2,384,384]{4,3,2,1,0:T(8,128)(2,1)} %green.3) | copy-start | bytes 5308420
  31.3 23.0 %copy-start.5 = (s32[3]{0:T(128)S(1)}, s32[3]{0:T(128)}, u32[]{:S(2)}) copy-start(s32[3]{0:T(128)} %counts.3) | copy-start | bytes 40
  71.7 6.4 %collective-permute-start.3 = (bf16[16,3,48,128]{3,2,1,0:T(8,128)(2,1)S(1)}, bf16[16,3,48,128]{3,2,1,0:T(8,128)(2,1)S(1)}, u32[]{:S(2)}, u32[]{:S(2)}) collective-permute-start(bf16[16,3,48,128]{3,2,1,0:T(8,128)(2,1)S(1)} %all_to_all.22.own), channel_id=1, source_target_pairs={{0,16},{16,0},{32,48},{48,32},{64,80},{80,64},{96,112},{112,96},{1... | collective-permute-start | bytes 1769480 | tf_op jit(solution)/shard_map/ppermute | solution.py:226
  75.3 12.4 %collective-permute-start.2 = (bf16[16,3,48,128]{3,2,1,0:T(8,128)(2,1)S(1)}, bf16[16,3,48,128]{3,2,1,0:T(8,128)(2,1)S(1)}, u32[]{:S(2)}, u32[]{:S(2)}) collective-permute-start(bf16[16,3,48,128]{3,2,1,0:T(8,128)(2,1)S(1)} %all_to_all.22.own), channel_id=1, source_target_pairs={{16,32},{32,16},{48,64},{64,48},{80,96},{96,80},{112,128},{128,112... | collective-permute-start | bytes 1769480 | tf_op jit(solution)/shard_map/ppermute | solution.py:225

commit v2 on v1

--- a/solution.py
+++ b/solution.py
@@ -7,6 +7,7 @@
 from jax.experimental.pallas import tpu as pltpu
 from jax.sharding import PartitionSpec as P
 
+
 ITERS = 2
 F32 = jnp.float32
 BF16 = jnp.bfloat16
@@ -16,12 +17,12 @@
 
 def coupling_kernel(span, odd, offsets, table, pairs, out):
     modes, momenta = pairs.shape[0], pairs.shape[1]
-    window = 3 * span
-    order = lax.broadcasted_iota(jnp.int32, (momenta, window * momenta), 0)
-    column = lax.broadcasted_iota(jnp.int32, (momenta, window * momenta), 1)
-    energy = lax.div(column, momenta)
-    mirrored = energy + jnp.where(energy < span, 2 * span, jnp.where(energy < 2 * span, 0, -2 * span))
-    energy = jnp.where(odd[0] == 1, mirrored, energy)
+    order = lax.broadcasted_iota(jnp.int32, (momenta, 3 * span * momenta), 0)
+    column = lax.broadcasted_iota(jnp.int32, (momenta, 3 * span * momenta), 1)
+    third = lax.div(column, span * momenta)
+    inside = lax.rem(lax.div(column, momenta), span)
+    below = jnp.where(odd[0] == 1, 1, 2)
+    energy = inside + jnp.where(third == 0, span, jnp.where(third == below, 0, 2 * span))
     spread = (lax.rem(column, momenta) == order).astype(F32)
     wide = []
     for m in range(modes):
@@ -89,24 +90,44 @@
         sent[:, e] = flat.reshape(sent.shape[0], sent.shape[2], sent.shape[3])
 
 
-def next_kernel(counts, green, contact, phonon, sent, kept):
+def next_kernel(counts, green, contact, phonon, sent):
     for e in range(green.shape[0]):
         back = phonon[:, e].reshape(contact.shape[2:])
         sigma = (contact[e, 0].astype(F32) + back.astype(F32)).astype(BF16)
         flat = lesser_point(green[e, 0], sigma, counts[e])
         sent[:, e] = flat.reshape(sent.shape[0], sent.shape[2], sent.shape[3])
-        kept[e, 0] = flat.reshape(kept.shape[2:])
-
-
-def mix_kernel(span, matrix, across, own, beside, out, turned, mixed):
-    momenta, rows = own.shape[0], own.shape[2]
-    for part, source in enumerate((across, own, beside)):
-        for i in range(span):
-            at = (part * span + i) * momenta
-            turned[:, at : at + momenta, :] = jnp.swapaxes(source[:, i], 0, 1)
+
+
+def turn(source, turned, start):
+    momenta, span = source.shape[0], source.shape[1]
+    for i in range(span):
+        at = start + i * momenta
+        turned[:, at : at + momenta, :] = jnp.swapaxes(source[:, i], 0, 1)
+
+
+def turn_kernel(own, beside, turned):
+    turn(own, turned, 0)
+    turn(beside, turned, own.shape[0] * own.shape[1])
+
+
+def turn_keep_kernel(own, beside, sent, turned, kept, sems):
+    copies = []
+    for e in range(sent.shape[1]):
+        copies.append(pltpu.make_async_copy(sent.at[:, e], kept.at[e], sems.at[e]))
+        copies[-1].start()
+    turn_kernel(own, beside, turned)
+    for copy in copies:
+        copy.wait()
+
+
+def mix_kernel(matrix, near, across, out, far, mixed):
+    momenta, span, rows = across.shape[0], across.shape[1], across.shape[2]
+    turn(across, far, 0)
     half = span * momenta
     for r in range(0, rows, 2):
-        right = jnp.concatenate([turned[r], turned[r + 1]], axis=1)
+        right = jnp.concatenate(
+            [jnp.concatenate([near[r], far[r]], axis=0), jnp.concatenate([near[r + 1], far[r + 1]], axis=0)], axis=1
+        )
         both = jnp.dot(matrix[...], right, preferred_element_type=F32)
         both = (both[:half] + both[half:]).astype(BF16)
         mixed[r] = both[:, : right.shape[1] // 2]
@@ -115,10 +136,15 @@
         out[:, j] = jnp.swapaxes(mixed[:, j * momenta : (j + 1) * momenta, :], 0, 1)
 
 
-def total_kernel(contact, phonon, out):
+def total_kernel(contact, phonon, out, summed, sems):
+    copies = []
     for e in range(contact.shape[0]):
         back = phonon[:, e].reshape(contact.shape[2:])
-        out[e, 0] = (contact[e, 0].astype(F32) + back.astype(F32)).astype(BF16)
+        summed[e, 0] = (contact[e, 0].astype(F32) + back.astype(F32)).astype(BF16)
+        copies.append(pltpu.make_async_copy(summed.at[e], out.at[e], sems.at[e]))
+        copies[-1].start()
+    for copy in copies:
+        copy.wait()
 
 
 def couplings(span, odd, offsets, table, pairs):
@@ -165,31 +191,58 @@
     vmem = pl.BlockSpec(memory_space=pltpu.VMEM)
     return pl.pallas_call(
         next_kernel,
-        out_shape=(chunks_of(contact, momenta), jax.ShapeDtypeStruct(contact.shape, BF16)),
+        out_shape=chunks_of(contact, momenta),
         in_specs=[pl.BlockSpec(memory_space=pltpu.SMEM), vmem, vmem, vmem],
-        out_specs=(vmem, vmem),
+        out_specs=vmem,
         name="lesser_next",
         compiler_params=PARAMS,
         cost_estimate=LESSER_COST,
     )(counts, green, contact, phonon)
 
 
-def mix(matrix, across, own, beside):
+def turn_near(own, beside, sent=None):
     momenta, span, rows, width = own.shape
     vmem = pl.BlockSpec(memory_space=pltpu.VMEM)
-    return pl.pallas_call(
-        functools.partial(mix_kernel, span),
-        out_shape=jax.ShapeDtypeStruct(own.shape, BF16),
-        in_specs=[vmem] * 4,
+    turned = jax.ShapeDtypeStruct((rows, 2 * span * momenta, width), BF16)
+    cost = pl.CostEstimate(flops=1_000_000, bytes_accessed=2_400_000, transcendentals=0)
+    if sent is None:
+        return pl.pallas_call(
+            turn_kernel,
+            out_shape=turned,
+            in_specs=[vmem, vmem],
+            out_specs=vmem,
+            name="turn",
+            compiler_params=PARAMS,
+            cost_estimate=cost,
+        )(own, beside)
+    return pl.pallas_call(
+        turn_keep_kernel,
+        out_shape=(turned, jax.ShapeDtypeStruct((span, momenta, rows, width), BF16)),
+        in_specs=[vmem, vmem, vmem],
+        out_specs=(vmem, pl.BlockSpec(memory_space=pltpu.HBM)),
+        scratch_shapes=[pltpu.SemaphoreType.DMA((span,))],
+        name="turn_keep",
+        compiler_params=PARAMS,
+        cost_estimate=cost,
+    )(own, beside, sent)
+
+
+def mix(matrix, near, across):
+    momenta, span, rows, width = across.shape
+    vmem = pl.BlockSpec(memory_space=pltpu.VMEM)
+    return pl.pallas_call(
+        mix_kernel,
+        out_shape=jax.ShapeDtypeStruct(across.shape, BF16),
+        in_specs=[vmem] * 3,
         out_specs=vmem,
         scratch_shapes=[
-            pltpu.VMEM((rows, 3 * span * momenta, width), BF16),
+            pltpu.VMEM((rows, span * momenta, width), BF16),
             pltpu.VMEM((rows, span * momenta, width), BF16),
         ],
         name="mix",
         compiler_params=PARAMS,
         cost_estimate=pl.CostEstimate(flops=200_000_000, bytes_accessed=2_400_000, transcendentals=0),
-    )(matrix, across, own, beside)
+    )(matrix, near, across)
 
 
 def total(contact, phonon):
@@ -198,7 +251,8 @@
         total_kernel,
         out_shape=jax.ShapeDtypeStruct(contact.shape, BF16),
         in_specs=[vmem, vmem],
-        out_specs=vmem,
+        out_specs=pl.BlockSpec(memory_space=pltpu.HBM),
+        scratch_shapes=[pltpu.VMEM(contact.shape, BF16), pltpu.SemaphoreType.DMA((contact.shape[0],))],
         name="total",
         compiler_params=PARAMS,
     )(contact, phonon)
@@ -220,12 +274,16 @@
     sent = first_lesser(*held, momenta)
     for sweep in range(ITERS):
         if sweep > 0:
-            sent, kept = next_lesser(tile_count, green, contact, phonon, momenta)
+            sent = next_lesser(tile_count, green, contact, phonon, momenta)
         own = exchange(sent)
         across = lax.ppermute(own, "energy", odd)
         beside = lax.ppermute(own, "energy", even)
-        phonon = exchange(mix(matrix, across, own, beside))
-    return kept, total(contact, phonon)
+        if sweep < ITERS - 1:
+            near = turn_near(own, beside)
+        else:
+            near, kept = turn_near(own, beside, sent)
+        phonon = exchange(mix(matrix, near, across))
+    return kept.reshape(contact.shape), total(contact, phonon)
 
 
 def solution(mesh):

time: 105 us -> 104 us (level)
  the two profiles are of different devices: /device:TPU:481 before, /device:TPU:865 now
where the time goes in v2:
time: 104 us; the launch traced here: 103 us
  blocking collectives  62.4 us (60%)
  waiting for transfers between devices  18.3 us (18%)
  starting transfers between devices  11.9 us (11%)
  Pallas kernels  9.89 us (10%)
    all_to_all x4, blocking collectives, exchange(): lax.all_to_all(block, 'momentum', split_axis=0, concat_axis=0, tiled=True)  62.4 us
    ppermute x2, waiting for transfers between devices, body(): across = lax.ppermute(own, 'energy', odd)  18.3 us
    ppermute x2, starting transfers between devices, body(): beside = lax.ppermute(own, 'energy', even)  7.39 us
    ppermute x2, starting transfers between devices, body(): across = lax.ppermute(own, 'energy', odd)  4.46 us
    pallas_call x1, Pallas kernels, first_lesser(): pl.pallas_call(first_kernel, out_shape=chunks_of(contact, momenta), in_sp...  3.42 us
    pallas_call x1, Pallas kernels, next_lesser(): pl.pallas_call(next_kernel, out_shape=chunks_of(contact, momenta), in_spe...  2.23 us
  transfers between devices with their start and end apart: 4, of which 2 were waited for; matrix products, arithmetic and copies ran while one was open for 0% of the time, Pallas kernels for 2%

profile of v2, /device:TPU:865, one launch (start us, length us, event | category | flops | bytes accessed | tf_op | source)
XLA Modules:
  0.0 103.2 jit_solution(5385160105134468615)
XLA Ops:
  0.6 3.4 %lesser_first.1 = bf16[16,3,48,128]{3,2,1,0:T(8,128)(2,1)S(1)} custom-call(s32[3]{0:T(128)} %counts.3, bf16[3,1,2,384,384]{4,3,2,1,0:T(8,128)(2,1)} %green.3, bf16[3,1,2,3,128,128]{5,4,3,2,1,0:T(8,128)(2,1)} %contact.5), custom_call_target="tpu_custom_call" | custom-call | flops 900000000 | bytes 4000000 | tf_op jit(solution)/shard_map/lesser_first/pallas_call | solution.py:173
  4.1 0.0 copy-start.2
  4.1 0.0 copy-start.3
  4.1 0.0 copy-start.4
  4.1 18.0 %all_to_all.20.own = bf16[16,3,48,128]{3,2,1,0:T(8,128)(2,1)S(1)} all-to-all(bf16[16,3,48,128]{3,2,1,0:T(8,128)(2,1)S(1)} %lesser_first.1), channel_id=1, replica_groups=mesh['energy'=64,'momentum'=16] {'momentum'}, dimensions={0} | all-to-all | bytes 1179648 | tf_op jit(solution)/shard_map/all_to_all | solution.py:262
  22.1 3.8 %collective-permute-start = (bf16[16,3,48,128]{3,2,1,0:T(8,128)(2,1)S(1)}, bf16[16,3,48,128]{3,2,1,0:T(8,128)(2,1)S(1)}, u32[]{:S(2)}, u32[]{:S(2)}) collective-permute-start(bf16[16,3,48,128]{3,2,1,0:T(8,128)(2,1)S(1)} %all_to_all.20.own), channel_id=1, source_target_pairs={{0,16},{16,0},{32,48},{48,32},{64,80},{80,64},{96,112},{112,96},{1... | collective-permute-start | bytes 1769480 | tf_op jit(solution)/shard_map/ppermute | solution.py:280
  25.9 2.5 %collective-permute-start.1 = (bf16[16,3,48,128]{3,2,1,0:T(8,128)(2,1)S(1)}, bf16[16,3,48,128]{3,2,1,0:T(8,128)(2,1)S(1)}, u32[]{:S(2)}, u32[]{:S(2)}) collective-permute-start(bf16[16,3,48,128]{3,2,1,0:T(8,128)(2,1)S(1)} %all_to_all.20.own), channel_id=1, source_target_pairs={{16,32},{32,16},{48,64},{64,48},{80,96},{96,80},{112,128},{128,112... | collective-permute-start | bytes 1769480 | tf_op jit(solution)/shard_map/ppermute | solution.py:279
  28.5 0.0 copy-done.2
  28.5 0.0 copy-done.3
  28.5 0.0 copy-done.4
  28.5 0.8 couplings.1.matrix
  29.3 0.0 collective-permute-done.beside
  29.3 0.4 turn.1.near
  29.7 8.7 %collective-permute-done.1.across = bf16[16,3,48,128]{3,2,1,0:T(8,128)(2,1)S(1)} collective-permute-done((bf16[16,3,48,128]{3,2,1,0:T(8,128)(2,1)S(1)}, bf16[16,3,48,128]{3,2,1,0:T(8,128)(2,1)S(1)}, u32[]{:S(2)}, u32[]{:S(2)}) %collective-permute-start.1) | collective-permute-done | bytes 589856 | tf_op jit(solution)/shard_map/ppermute | solution.py:279
  38.3 0.0 copy-start.1
  38.3 0.7 mix.2
  39.0 0.0 copy-start
  39.0 0.0 copy-start.5
  39.0 15.1 %all_to_all.21.phonon = bf16[16,3,48,128]{3,2,1,0:T(8,128)(2,1)S(1)} all-to-all(bf16[16,3,48,128]{3,2,1,0:T(8,128)(2,1)S(1)} %mix.2), channel_id=1, replica_groups=mesh['energy'=64,'momentum'=16] {'momentum'}, dimensions={0} | all-to-all | bytes 1179648 | tf_op jit(solution)/shard_map/all_to_all | solution.py:262
  54.1 0.0 copy-done.1
  54.1 0.0 copy-done
  54.1 0.0 copy-done.5
  54.1 2.2 %lesser_next.1.sent = bf16[16,3,48,128]{3,2,1,0:T(8,128)(2,1)S(1)} custom-call(s32[3]{0:T(128)S(1)} %copy-done.5, bf16[3,1,2,384,384]{4,3,2,1,0:T(8,128)(2,1)S(1)} %copy-done.1, bf16[3,1,2,3,128,128]{5,4,3,2,1,0:T(8,128)(2,1)S(1)} %copy-done, bf16[16,3,48,128]{3,2,1,0:T(8,128)(2,1)S(1)} %all_to_all.21.phonon), custom_call_target="tpu_custom_call" | custom-call | flops 900000000 | bytes 4000000 | tf_op jit(solution)/shard_map/lesser_next/pallas_call | solution.py:192
  56.3 14.4 %all_to_all.22.own = bf16[16,3,48,128]{3,2,1,0:T(8,128)(2,1)S(1)} all-to-all(bf16[16,3,48,128]{3,2,1,0:T(8,128)(2,1)S(1)} %lesser_next.1.sent), channel_id=1, replica_groups=mesh['energy'=64,'momentum'=16] {'momentum'}, dimensions={0} | all-to-all | bytes 1179648 | tf_op jit(solution)/shard_map/all_to_all | solution.py:262
  70.7 3.6 %collective-permute-start.2 = (bf16[16,3,48,128]{3,2,1,0:T(8,128)(2,1)S(1)}, bf16[16,3,48,128]{3,2,1,0:T(8,128)(2,1)S(1)}, u32[]{:S(2)}, u32[]{:S(2)}) collective-permute-start(bf16[16,3,48,128]{3,2,1,0:T(8,128)(2,1)S(1)} %all_to_all.22.own), channel_id=1, source_target_pairs={{0,16},{16,0},{32,48},{48,32},{64,80},{80,64},{96,112},{112,96},{1... | collective-permute-start | bytes 1769480 | tf_op jit(solution)/shard_map/ppermute | solution.py:280
  74.3 1.9 %collective-permute-start.3 = (bf16[16,3,48,128]{3,2,1,0:T(8,128)(2,1)S(1)}, bf16[16,3,48,128]{3,2,1,0:T(8,128)(2,1)S(1)}, u32[]{:S(2)}, u32[]{:S(2)}) collective-permute-start(bf16[16,3,48,128]{3,2,1,0:T(8,128)(2,1)S(1)} %all_to_all.22.own), channel_id=1, source_target_pairs={{16,32},{32,16},{48,64},{64,48},{80,96},{96,80},{112,128},{128,112... | collective-permute-start | bytes 1769480 | tf_op jit(solution)/shard_map/ppermute | solution.py:279
  76.3 0.0 collective-permute-done.2.beside
  76.3 0.8 turn_keep.1
  77.1 9.6 %collective-permute-done.3.across = bf16[16,3,48,128]{3,2,1,0:T(8,128)(2,1)S(1)} collective-permute-done((bf16[16,3,48,128]{3,2,1,0:T(8,128)(2,1)S(1)}, bf16[16,3,48,128]{3,2,1,0:T(8,128)(2,1)S(1)}, u32[]{:S(2)}, u32[]{:S(2)}) %collective-permute-start.3) | collective-permute-done | bytes 589856 | tf_op jit(solution)/shard_map/ppermute | solution.py:279
  86.7 0.7 mix.3
  87.4 14.9 %all_to_all.23.phonon = bf16[16,3,48,128]{3,2,1,0:T(8,128)(2,1)S(1)} all-to-all(bf16[16,3,48,128]{3,2,1,0:T(8,128)(2,1)S(1)} %mix.3), channel_id=1, replica_groups=mesh['energy'=64,'momentum'=16] {'momentum'}, dimensions={0} | all-to-all | bytes 1179648 | tf_op jit(solution)/shard_map/all_to_all | solution.py:262
  102.4 0.9 total.1
Async XLA Ops:
  4.1 24.4 %copy-start.2 = (s32[3,16,16]{2,1,0:T(8,128)S(1)}, s32[3,16,16]{2,1,0:T(8,128)}, u32[]{:S(2)}) copy-start(s32[3,16,16]{2,1,0:T(8,128)} %pairs.1) | copy-start | bytes 9220
  4.1 24.4 %copy-start.3 = (f32[3,16]{1,0:T(4,128)S(1)}, f32[3,16]{1,0:T(4,128)}, u32[]{:S(2)}) copy-start(f32[3,16]{1,0:T(4,128)} %table.1) | copy-start | bytes 580
  4.1 24.4 %copy-start.4 = (s32[3]{0:T(128)S(1)}, s32[3]{0:T(128)}, u32[]{:S(2)}) copy-start(s32[3]{0:T(128)} %offsets.1) | copy-start | bytes 40
  22.1 7.2 %collective-permute-start = (bf16[16,3,48,128]{3,2,1,0:T(8,128)(2,1)S(1)}, bf16[16,3,48,128]{3,2,1,0:T(8,128)(2,1)S(1)}, u32[]{:S(2)}, u32[]{:S(2)}) collective-permute-start(bf16[16,3,48,128]{3,2,1,0:T(8,128)(2,1)S(1)} %all_to_all.20.own), channel_id=1, source_target_pairs={{0,16},{16,0},{32,48},{48,32},{64,80},{80,64},{96,112},{112,96},{1... | collective-permute-start | bytes 1769480 | tf_op jit(solution)/shard_map/ppermute | solution.py:280
  25.9 12.4 %collective-permute-start.1 = (bf16[16,3,48,128]{3,2,1,0:T(8,128)(2,1)S(1)}, bf16[16,3,48,128]{3,2,1,0:T(8,128)(2,1)S(1)}, u32[]{:S(2)}, u32[]{:S(2)}) collective-permute-start(bf16[16,3,48,128]{3,2,1,0:T(8,128)(2,1)S(1)} %all_to_all.20.own), channel_id=1, source_target_pairs={{16,32},{32,16},{48,64},{64,48},{80,96},{96,80},{112,128},{128,112... | collective-permute-start | bytes 1769480 | tf_op jit(solution)/shard_map/ppermute | solution.py:279
  38.3 15.8 %copy-start.1 = (bf16[3,1,2,384,384]{4,3,2,1,0:T(8,128)(2,1)S(1)}, bf16[3,1,2,384,384]{4,3,2,1,0:T(8,128)(2,1)}, u32[]{:S(2)}) copy-start(bf16[3,1,2,384,384]{4,3,2,1,0:T(8,128)(2,1)} %green.3) | copy-start | bytes 5308420
  39.0 15.1 %copy-start = (bf16[3,1,2,3,128,128]{5,4,3,2,1,0:T(8,128)(2,1)S(1)}, bf16[3,1,2,3,128,128]{5,4,3,2,1,0:T(8,128)(2,1)}, u32[]{:S(2)}) copy-start(bf16[3,1,2,3,128,128]{5,4,3,2,1,0:T(8,128)(2,1)} %contact.5) | copy-start | bytes 1769476
  39.0 15.1 %copy-start.5 = (s32[3]{0:T(128)S(1)}, s32[3]{0:T(128)}, u32[]{:S(2)}) copy-start(s32[3]{0:T(128)} %counts.3) | copy-start | bytes 40
  70.7 5.5 %collective-permute-start.2 = (bf16[16,3,48,128]{3,2,1,0:T(8,128)(2,1)S(1)}, bf16[16,3,48,128]{3,2,1,0:T(8,128)(2,1)S(1)}, u32[]{:S(2)}, u32[]{:S(2)}) collective-permute-start(bf16[16,3,48,128]{3,2,1,0:T(8,128)(2,1)S(1)} %all_to_all.22.own), channel_id=1, source_target_pairs={{0,16},{16,0},{32,48},{48,32},{64,80},{80,64},{96,112},{112,96},{1... | collective-permute-start | bytes 1769480 | tf_op jit(solution)/shard_map/ppermute | solution.py:280
  74.3 12.4 %collective-permute-start.3 = (bf16[16,3,48,128]{3,2,1,0:T(8,128)(2,1)S(1)}, bf16[16,3,48,128]{3,2,1,0:T(8,128)(2,1)S(1)}, u32[]{:S(2)}, u32[]{:S(2)}) collective-permute-start(bf16[16,3,48,128]{3,2,1,0:T(8,128)(2,1)S(1)} %all_to_all.22.own), channel_id=1, source_target_pairs={{16,32},{32,16},{48,64},{64,48},{80,96},{96,80},{112,128},{128,112... | collective-permute-start | bytes 1769480 | tf_op jit(solution)/shard_map/ppermute | solution.py:279
